TPU v7x, 128 devices: a whole 4x4x4 slice. The times are simulated.
128 devices in a mesh: row: 8 (over y, core), col: 16 (over x, z).
Axes of the slice: x: 4, y: 4, z: 4, core: 2. Of those that a mesh axis runs over, the one named last changes fastest.
Arguments:
- tokens: bfloat16 [1024, 8192], P('row', 'col'), may hold values from -6 to 6
- gate_weight: bfloat16 [8192, 28672], P('col', 'row'), may hold values from -0.09375 to 0.09375
- up_weight: bfloat16 [8192, 28672], P('col', 'row'), may hold values from -0.09375 to 0.09375
- down_weight: bfloat16 [28672, 8192], P('row', 'col'), may hold values from -0.046875 to 0.046875
- gate_mask: int32 [64, 224], P('col', 'row'), may hold values 0 or 1
- up_mask: int32 [64, 224], P('col', 'row'), may hold values 0 or 1
- down_mask: int32 [224, 64], P('row', 'col'), may hold values 0 or 1
Outputs:
- mixed_out: bfloat16 [1024, 8192], P('row', 'col')
Inputs may be any that keep to these rules, and one draw needn't show every extreme that they name: `gate_mask`: each entry keeps (1) or drops (0) one block. `up_mask`: each entry keeps (1) or drops (0) one block. `down_mask`: each entry keeps (1) or drops (0) one block.
All inputs are finite; a program needn't handle non-finite values.
Results may differ from a plain program's by a relative error of at most 0.025.
Values may be sent and summed in bfloat16 or wider, within the bound.
A program may use at most 128 MiB of HBM per device.

v0:
```python
import jax
import jax.numpy as jnp
from jax import lax
from jax.sharding import PartitionSpec as P


def expand(weight, block_mask):
    row_count, col_count = weight.shape
    mask_rows, mask_cols = block_mask.shape
    shaped = weight.reshape(mask_rows, row_count // mask_rows, mask_cols, col_count // mask_cols)
    kept_blocks = shaped * block_mask.astype(weight.dtype)[:, None, :, None]
    return kept_blocks.reshape(row_count, col_count)


def per_device(tokens, gate_weight, up_weight, down_weight, gate_mask, up_mask, down_mask):
    kept_gate = expand(gate_weight, gate_mask)
    kept_up = expand(up_weight, up_mask)
    kept_down = expand(down_weight, down_mask)
    gathered = lax.all_gather(tokens, "row", axis=0, tiled=True)
    gate_part = jnp.dot(gathered, kept_gate, preferred_element_type=jnp.float32)
    up_part = jnp.dot(gathered, kept_up, preferred_element_type=jnp.float32)
    gate_sum, up_sum = (
        lax.psum(gate_part.astype(jnp.bfloat16), "col").astype(jnp.float32),
        lax.psum(up_part.astype(jnp.bfloat16), "col").astype(jnp.float32),
    )
    hidden = (jax.nn.silu(gate_sum) * up_sum).astype(jnp.bfloat16)
    return lax.psum_scatter(
        jnp.dot(hidden, kept_down, preferred_element_type=jnp.float32).astype(jnp.bfloat16),
        "row",
        scatter_dimension=0,
        tiled=True,
    )


def solution(mesh):
    return jax.shard_map(
        per_device,
        mesh=mesh,
        in_specs=(
            P("row", "col"),
            P("col", "row"),
            P("col", "row"),
            P("row", "col"),
            P("col", "row"),
            P("col", "row"),
            P("row", "col"),
        ),
        out_specs=P("row", "col"),
        check_vma=False,
    )
```

profile of v0, /device:TPU:0, one launch (start us, length us, event | category | flops | bytes accessed | tf_op | source)
XLA Modules:
  0.0 304.0 jit_solution(16321837674155461157)
XLA Ops:
  6.5 0.0 all-gather.2.cloned.1.call-start
  6.5 0.7 all-gather.2.cloned.1.call-update
  7.3 0.0 all-reduce.3.cloned.1.call-start
  7.3 0.7 convert_element_type.33
  8.0 0.1 copy.9
  8.1 0.0 copy-start.2
  8.1 6.0 %copy.10 = bf16[512,3584]{0,1:T(8,128)(2,1)} copy(bf16[512,3584]{1,0:T(8,128)(2,1)} %param.8) | data formatting | bytes 7340032 | tf_op args[1]
  14.1 0.0 copy-done.2
  14.1 0.1 copy.11
  14.2 5.9 %copy.12 = bf16[512,3584]{0,1:T(8,128)(2,1)} copy(bf16[512,3584]{1,0:T(8,128)(2,1)} %param.9) | data formatting | bytes 7340032 | tf_op args[2]
  20.1 14.7 %all-gather.2.cloned.1.call-done = bf16[1024,512]{1,0:T(8,128)(2,1)} async-done(((bf16[128,512]{1,0:T(8,128)(2,1)}), bf16[1024,512]{1,0:T(8,128)(2,1)}) %all-gather.2.cloned.1.call-update) | async-done | bytes 1048592 | tf_op jit(solution)/shard_map/all_gather | solution.py:19
  34.8 0.0 copy-start.1
  34.8 1.0 mul.40
  35.8 1.0 copy-done.1
  36.9 0.0 copy-start.5
  36.9 7.4 %fusion.7 = bf16[1024,3584]{0,1:T(8,128)(2,1)} fusion(bf16[1024,512]{1,0:T(8,128)(2,1)} %all-gather.2.cloned.1.call-done, bf16[512,3584]{0,1:T(8,128)(2,1)S(1)} %copy-done.1, bf16[448,8,4,128]{3,2,1,0:T(4,128)(2,1)S(1)} %bitcast.29), kind=kOutput, calls=%fused_computation.10 | convolution fusion | flops 3763601408 | bytes 15728640 | tf_op jit(solution)/shard_map/dot_general | solution.py:20
  44.3 0.0 copy-start
  44.3 1.0 mul.44
  45.3 0.0 copy-done.5
  45.3 1.0 copy-done
  46.4 6.1 %fusion.8 = bf16[1024,3584]{0,1:T(8,128)(2,1)} fusion(bf16[1024,512]{1,0:T(8,128)(2,1)S(1)} %copy-done.5, bf16[512,3584]{0,1:T(8,128)(2,1)S(1)} %copy-done, bf16[448,8,4,128]{3,2,1,0:T(4,128)(2,1)S(1)} %bitcast.27), kind=kOutput, calls=%fused_computation.11 | convolution fusion | flops 3763601408 | bytes 15728640 | tf_op jit(solution)/shard_map/dot_general | solution.py:21
  52.4 0.0 copy-start.3
  52.4 0.0 all-reduce.3.cloned.1.call-update
  52.5 0.0 reduce-scatter.2.cloned.1.call-start
  52.5 0.6 copy-done.3
  53.1 0.1 copy.13
  53.2 198.4 %all-reduce.3.cloned.1.call-done = (bf16[1024,3584]{0,1:T(8,128)(2,1)}, bf16[1024,3584]{0,1:T(8,128)(2,1)}) async-done(((bf16[1024,3584]{0,1:T(8,128)(2,1)}, bf16[1024,3584]{0,1:T(8,128)(2,1)}), (bf16[1024,3584]{0,1:T(8,128)(2,1)}, bf16[1024,3584]{0,1:T(8,128)(2,1)})) %all-reduce.3.cloned.1.call-update) | async-done | bytes 14680080 | tf_op jit(solution)/shard_map/psum | solution.py:24
  251.6 1.0 mul.48
  252.7 1.0 copy-done.4
  253.7 11.6 %fusion.12 = bf16[1024,512]{1,0:T(8,128)(2,1)} fusion(bf16[3584,512]{1,0:T(8,128)(2,1)S(1)} %copy-done.4, bf16[448,8,4,128]{3,2,1,0:T(4,128)(2,1)S(1)} %bitcast.28, bf16[1024,3584]{0,1:T(8,128)(2,1)} %get-tuple-element.5, bf16[1024,3584]{0,1:T(8,128)(2,1)} %get-tuple-element.6), kind=kOutput, calls=%fused_computation.18 | convolution fusion | flops 3789815808 | bytes 23068672 | tf_op jit(solution)/shard_map/dot_general | solution.py:28
  265.3 0.0 reduce-scatter.2.cloned.1.call-update
  265.3 32.1 %reduce-scatter.2.cloned.1.call-done = bf16[128,512]{1,0:T(8,128)(2,1)} async-done(((bf16[1024,512]{1,0:T(8,128)(2,1)}), bf16[128,512]{1,0:T(8,128)(2,1)}) %reduce-scatter.2.cloned.1.call-update) | async-done | bytes 131088 | tf_op jit(solution)/shard_map/reduce_scatter | solution.py:27
  (3 shorter events, 0.0 us)
Async XLA Ops:
  6.5 28.3 %all-gather.2.cloned.1.call-start = ((), (), s32[]{:S(2)}) async-start(), calls=%async_computation.1 | async-start | bytes 1179648 | tf_op jit(solution)/shard_map/all_gather | solution.py:19
  7.3 244.4 %all-reduce.3.cloned.1.call-start = ((), (), s32[]{:S(2)}) async-start(), calls=%async_computation.3 | async-start | bytes 29360128 | tf_op jit(solution)/shard_map/psum | solution.py:24
  8.1 6.0 %copy-start.2 = (s32[4,28]{1,0:T(4,128)S(1)}, s32[4,28]{1,0:T(4,128)}, u32[]{:S(2)}) copy-start(s32[4,28]{1,0:T(4,128)} %param.12) | copy-start | bytes 1348
  34.8 2.0 copy-start.1
  36.9 8.5 %copy-start.5 = (bf16[1024,512]{1,0:T(8,128)(2,1)S(1)}, bf16[1024,512]{1,0:T(8,128)(2,1)}, u32[]{:S(2)}) copy-start(bf16[1024,512]{1,0:T(8,128)(2,1)} %all-gather.2.cloned.1.call-done) | copy-start | bytes 3145732
  44.3 2.0 copy-start
  52.4 0.7 copy-start.3
  52.5 245.0 %reduce-scatter.2.cloned.1.call-start = ((), (), s32[]{:S(2)}) async-start(), calls=%async_computation.2 | async-start | bytes 1179648 | tf_op jit(solution)/shard_map/reduce_scatter | solution.py:27
  251.6 2.0 copy-start.4
Sparse Core Ops, SparseCore 0:
  9.0 25.7 all-gather.1
  52.6 199.0 all-reduce.2
  265.4 31.9 reduce-scatter.1
where the time goes:
time: 304 us
  waiting for transfers between devices  246 us (81%)
  matrix products  25.1 us (8%)
  local copies, waits for them, and re-layouts  18.9 us (6%)
  between operations  13.1 us (4%)
    psum x1, waiting for transfers between devices, per_device(): lax.psum(up_part.astype(jnp.bfloat16), 'col').astype(jnp.float32)  198 us
    reduce_scatter x1, waiting for transfers between devices, per_device(): lax.psum_scatter(jnp.dot(hidden, kept_down, preferred_element_type=jnp.fl...  32.1 us
    unnamed x14, local copies, waits for them, and re-layouts  15.6 us
    all_gather x1, waiting for transfers between devices, per_device(): gathered = lax.all_gather(tokens, 'row', axis=0, tiled=True)  14.7 us
    dot_general x1, matrix products, per_device(): jnp.dot(hidden, kept_down, preferred_element_type=jnp.float32)  11.6 us
    dot_general x1, matrix products, per_device(): gate_part = jnp.dot(gathered, kept_gate, preferred_element_type=jnp.float32)  7.45 us
    dot_general x1, matrix products, per_device(): up_part = jnp.dot(gathered, kept_up, preferred_element_type=jnp.float32)  6.08 us
  transfers between devices with their start and end apart: 3, of which 3 were waited for; matrix products, arithmetic and copies ran while one was open for 4% of the time, Pallas kernels for 0%

commit v1 on v0

--- a/solution.py
+++ b/solution.py
@@ -16,7 +16,21 @@
     kept_gate = expand(gate_weight, gate_mask)
     kept_up = expand(up_weight, up_mask)
     kept_down = expand(down_weight, down_mask)
-    gathered = lax.all_gather(tokens, "row", axis=0, tiled=True)
+    ways, here, turn = (lax.axis_size("row"), lax.axis_index("row"), tokens.shape[0])
+    dims = [n * ways if d == 0 else n for d, n in enumerate(tokens.shape)]
+    full = lax.dynamic_update_slice_in_dim(
+        jnp.zeros(dims, tokens.dtype), tokens, here * turn, axis=0
+    )
+    going_up = going_down = tokens
+    for far in range(1, ways // 2 + 1):
+        going_up = lax.ppermute(going_up, "row", [(d, (d + 1) % ways) for d in range(ways)])
+        full = lax.dynamic_update_slice_in_dim(full, going_up, (here - far) % ways * turn, axis=0)
+        if 2 * far < ways:
+            going_down = lax.ppermute(going_down, "row", [(d, (d - 1) % ways) for d in range(ways)])
+            full = lax.dynamic_update_slice_in_dim(
+                full, going_down, (here + far) % ways * turn, axis=0
+            )
+    gathered = full
     gate_part = jnp.dot(gathered, kept_gate, preferred_element_type=jnp.float32)
     up_part = jnp.dot(gathered, kept_up, preferred_element_type=jnp.float32)
     gate_sum, up_sum = (

time: 304 us -> 305 us (level)
  starting transfers between devices: 0.08 us -> 8.91 us
  waiting for transfers between devices: 246 us -> 241 us
  matrix products: 25.1 us -> 21.9 us
    all_gather x1 -> x0, waiting for transfers between devices: 14.7 us -> none  [per_device(): gathered = lax.all_gather(tokens, 'row', axis=0, tiled=True)]
    ppermute x0 -> x7, waiting for transfers between devices: none -> 10.8 us  [the longest x4 10.8 us: per_device(): lax.ppermute(going_up, 'row', [(d, (d + 1) % ways) for d in range(ways)])]
    ppermute x0 -> x7, starting transfers between devices: none -> 8.87 us  [the longest x3 8.84 us: per_device(): lax.ppermute(going_down, 'row', [(d, (d - 1) % ways) for d in range(ways)])]
  transfers between devices with their start and end apart: 3 -> 9, of which waited for: 3 -> 5; matrix products, arithmetic and copies ran while one was open for 4% -> 4% of each run, Pallas kernels for 0% -> 0%
where the time goes in v1:
time: 305 us; the launch traced here: 304 us
  waiting for transfers between devices  241 us (79%)
  matrix products  21.9 us (7%)
  local copies, waits for them, and re-layouts  18.1 us (6%)
  between operations  13.5 us (4%)
  starting transfers between devices  8.91 us (3%)
    psum x1, waiting for transfers between devices, per_device(): lax.psum(up_part.astype(jnp.bfloat16), 'col').astype(jnp.float32)  198 us
    reduce_scatter x1, waiting for transfers between devices, per_device(): lax.psum_scatter(jnp.dot(hidden, kept_down, preferred_element_type=jnp.fl...  32.1 us
    unnamed x14, local copies, waits for them, and re-layouts  14.6 us
    ppermute x4, waiting for transfers between devices, per_device(): lax.ppermute(going_up, 'row', [(d, (d + 1) % ways) for d in range(ways)])  10.8 us
    dot_general x1, matrix products, per_device(): jnp.dot(hidden, kept_down, preferred_element_type=jnp.float32)  9.69 us
    ppermute x3, starting transfers between devices, per_device(): lax.ppermute(going_down, 'row', [(d, (d - 1) % ways) for d in range(ways)])  8.84 us
    dot_general x1, matrix products, per_device(): up_part = jnp.dot(gathered, kept_up, preferred_element_type=jnp.float32)  6.12 us
  transfers between devices with their start and end apart: 9, of which 5 were waited for; matrix products, arithmetic and copies ran while one was open for 4% of the time, Pallas kernels for 0%

profile of v1, /device:TPU:0, one launch (start us, length us, event | category | flops | bytes accessed | tf_op | source)
XLA Modules:
  0.0 304.3 jit_solution(14780556473474078986)
XLA Ops:
  6.5 0.0 collective-permute-start
  6.5 3.0 collective-permute-start.1
  9.5 0.7 convert_element_type.30
  10.2 0.1 copy.11
  10.3 5.9 %copy.12 = bf16[512,3584]{0,1:T(8,128)(2,1)} copy(bf16[512,3584]{1,0:T(8,128)(2,1)} %param.9) | data formatting | bytes 7340032 | tf_op args[2]
  16.2 0.1 copy.9
  16.4 6.0 %copy.10 = bf16[512,3584]{0,1:T(8,128)(2,1)} copy(bf16[512,3584]{1,0:T(8,128)(2,1)} %param.8) | data formatting | bytes 7340032 | tf_op args[1]
  22.3 0.1 broadcast_in_dim.2
  22.4 0.0 collective-permute-done
  22.5 0.0 collective-permute-start.2
  22.5 0.0 collective-permute-done.1
  22.5 2.9 collective-permute-start.3
  25.5 2.6 collective-permute-done.2
  28.1 0.0 collective-permute-done.3
  28.1 3.0 collective-permute-start.5
  31.1 2.6 collective-permute-done.4
  33.7 5.5 %collective-permute-done.6 = bf16[128,512]{1,0:T(8,128)(2,1)S(1)} collective-permute-done((bf16[128,512]{1,0:T(8,128)(2,1)S(1)}, bf16[128,512]{1,0:T(8,128)(2,1)S(1)}, u32[]{:S(2)}, u32[]{:S(2)}) %collective-permute-start.6) | collective-permute-done | bytes 131104 | tf_op jit(solution)/shard_map/ppermute | solution.py:26
  39.3 1.0 mul.76
  40.3 6.1 %convolution_convert_fusion = bf16[1024,3584]{1,0:T(8,128)(2,1)} fusion(bf16[1024,512]{1,0:T(8,128)(2,1)S(1)} %constant_dynamic-update-slice_fusion, bf16[512,3584]{0,1:T(8,128)(2,1)S(1)} %copy-done.1, bf16[448,8,4,128]{3,2,1,0:T(4,128)(2,1)S(1)} %bitcast.25), kind=kOutput, calls=%fused_computation.7 | convolution fusion | flops 3763601408 | bytes 15728640 | tf_op jit(solution)/shard_map/dot_general | solution.py:35
  46.4 1.0 mul.72
  47.5 1.0 copy-done
  48.5 6.1 %convolution_convert_fusion.1 = bf16[1024,3584]{1,0:T(8,128)(2,1)} fusion(bf16[1024,512]{1,0:T(8,128)(2,1)S(1)} %constant_dynamic-update-slice_fusion, bf16[512,3584]{0,1:T(8,128)(2,1)S(1)} %copy-done, bf16[448,8,4,128]{3,2,1,0:T(4,128)(2,1)S(1)} %bitcast.23), kind=kOutput, calls=%fused_computation.8 | convolution fusion | flops 3763601408 | bytes 15728640 | tf_op jit(solution)/shard_map/dot_general | solution.py:34
  54.6 0.0 all-reduce.3.cloned.1.call-update
  54.6 0.0 reduce-scatter.2.cloned.1.call-start
  54.6 0.6 copy-done.4
  55.2 0.1 copy.13
  55.4 198.3 %all-reduce.3.cloned.1.call-done = (bf16[1024,3584]{1,0:T(8,128)(2,1)}, bf16[1024,3584]{1,0:T(8,128)(2,1)}) async-done(((bf16[1024,3584]{1,0:T(8,128)(2,1)}, bf16[1024,3584]{1,0:T(8,128)(2,1)}), (bf16[1024,3584]{1,0:T(8,128)(2,1)}, bf16[1024,3584]{1,0:T(8,128)(2,1)})) %all-reduce.3.cloned.1.call-update) | async-done | bytes 14680080 | tf_op jit(solution)/shard_map/psum | solution.py:38
  253.7 1.0 mul.80
  254.7 1.0 copy-done.5
  255.7 9.7 %fusion.10 = bf16[1024,512]{1,0:T(8,128)(2,1)} fusion(bf16[3584,512]{1,0:T(8,128)(2,1)S(1)} %copy-done.5, bf16[448,8,4,128]{3,2,1,0:T(4,128)(2,1)S(1)} %bitcast.24, bf16[1024,3584]{1,0:T(8,128)(2,1)} %get-tuple-element.5, bf16[1024,3584]{1,0:T(8,128)(2,1)} %get-tuple-element.6), kind=kOutput, calls=%fused_computation.16 | convolution fusion | flops 3789815808 | bytes 23068672 | tf_op jit(solution)/shard_map/dot_general | solution.py:42
  265.4 0.0 reduce-scatter.2.cloned.1.call-update
  265.4 32.1 %reduce-scatter.2.cloned.1.call-done = bf16[128,512]{1,0:T(8,128)(2,1)} async-done(((bf16[1024,512]{1,0:T(8,128)(2,1)}), bf16[128,512]{1,0:T(8,128)(2,1)}) %reduce-scatter.2.cloned.1.call-update) | async-done | bytes 131088 | tf_op jit(solution)/shard_map/reduce_scatter | solution.py:41
  (23 shorter events, 0.2 us)
Async XLA Ops:
  6.5 247.1 %all-reduce.3.cloned.1.call-start = ((), (), s32[]{:S(2)}) async-start(), calls=%async_computation.2 | async-start | bytes 29360128 | tf_op jit(solution)/shard_map/psum | solution.py:38
  6.5 15.9 %collective-permute-start = (bf16[128,512]{1,0:T(8,128)(2,1)}, bf16[128,512]{1,0:T(8,128)(2,1)S(1)}, u32[]{:S(2)}, u32[]{:S(2)}) collective-permute-start(bf16[128,512]{1,0:T(8,128)(2,1)} %param.7), channel_id=1, source_target_pairs={{0,16},{16,32},{32,48},{48,64},{64,80},{80,96},{96,112},{112,0},{1... | collective-permute-start | bytes 393224 | tf_op jit(solution)/shard_map/ppermute | solution.py:26
  6.5 15.9 %collective-permute-start.1 = (bf16[128,512]{1,0:T(8,128)(2,1)}, bf16[128,512]{1,0:T(8,128)(2,1)S(1)}, u32[]{:S(2)}, u32[]{:S(2)}) collective-permute-start(bf16[128,512]{1,0:T(8,128)(2,1)} %param.7), channel_id=1, source_target_pairs={{0,112},{16,0},{32,16},{48,32},{64,48},{80,64},{96,80},{112,96},{1... | collective-permute-start | bytes 393224 | tf_op jit(solution)/shard_map/ppermute | solution.py:29
  10.3 5.9 %copy-start.3 = (s32[4,28]{1,0:T(4,128)S(1)}, s32[4,28]{1,0:T(4,128)}, u32[]{:S(2)}) copy-start(s32[4,28]{1,0:T(4,128)} %param.11) | copy-start | bytes 1348
  16.4 6.1 %copy-start.2 = (bf16[128,512]{1,0:T(8,128)(2,1)S(1)}, bf16[128,512]{1,0:T(8,128)(2,1)}, u32[]{:S(2)}) copy-start(bf16[128,512]{1,0:T(8,128)(2,1)} %param.7) | copy-start | bytes 393220
  22.3 18.0 %copy-start.1 = (bf16[512,3584]{0,1:T(8,128)(2,1)S(1)}, bf16[512,3584]{0,1:T(8,128)(2,1)}, u32[]{:S(2)}) copy-start(bf16[512,3584]{0,1:T(8,128)(2,1)} %copy.12) | copy-start | bytes 11010052
  22.5 5.6 %collective-permute-start.2 = (bf16[128,512]{1,0:T(8,128)(2,1)S(1)}, bf16[128,512]{1,0:T(8,128)(2,1)S(1)}, u32[]{:S(2)}, u32[]{:S(2)}) collective-permute-start(bf16[128,512]{1,0:T(8,128)(2,1)S(1)} %collective-permute-done), channel_id=1, source_target_pairs={{0,16},{16,32},{32,48},{48,64},{64,80},{80,96},{96,112},{112,0},{1... | collective-permute-start | bytes 393224 | tf_op jit(solution)/shard_map/ppermute | solution.py:26
  22.5 5.6 %collective-permute-start.3 = (bf16[128,512]{1,0:T(8,128)(2,1)S(1)}, bf16[128,512]{1,0:T(8,128)(2,1)S(1)}, u32[]{:S(2)}, u32[]{:S(2)}) collective-permute-start(bf16[128,512]{1,0:T(8,128)(2,1)S(1)} %collective-permute-done.1), channel_id=1, source_target_pairs={{0,112},{16,0},{32,16},{48,32},{64,48},{80,64},{96,80},{112,96},{1... | collective-permute-start | bytes 393224 | tf_op jit(solution)/shard_map/ppermute | solution.py:29
  28.1 5.6 %collective-permute-start.4 = (bf16[128,512]{1,0:T(8,128)(2,1)S(1)}, bf16[128,512]{1,0:T(8,128)(2,1)S(1)}, u32[]{:S(2)}, u32[]{:S(2)}) collective-permute-start(bf16[128,512]{1,0:T(8,128)(2,1)S(1)} %collective-permute-done.2), channel_id=1, source_target_pairs={{0,16},{16,32},{32,48},{48,64},{64,80},{80,96},{96,112},{112,0},{1... | collective-permute-start | bytes 393224 | tf_op jit(solution)/shard_map/ppermute | solution.py:26
  28.1 5.6 %collective-permute-start.5 = (bf16[128,512]{1,0:T(8,128)(2,1)S(1)}, bf16[128,512]{1,0:T(8,128)(2,1)S(1)}, u32[]{:S(2)}, u32[]{:S(2)}) collective-permute-start(bf16[128,512]{1,0:T(8,128)(2,1)S(1)} %collective-permute-done.3), channel_id=1, source_target_pairs={{0,112},{16,0},{32,16},{48,32},{64,48},{80,64},{96,80},{112,96},{1... | collective-permute-start | bytes 393224 | tf_op jit(solution)/shard_map/ppermute | solution.py:29
  33.7 5.6 %collective-permute-start.6 = (bf16[128,512]{1,0:T(8,128)(2,1)S(1)}, bf16[128,512]{1,0:T(8,128)(2,1)S(1)}, u32[]{:S(2)}, u32[]{:S(2)}) collective-permute-start(bf16[128,512]{1,0:T(8,128)(2,1)S(1)} %collective-permute-done.4), channel_id=1, source_target_pairs={{0,16},{16,32},{32,48},{48,64},{64,80},{80,96},{96,112},{112,0},{1... | collective-permute-start | bytes 393224 | tf_op jit(solution)/shard_map/ppermute | solution.py:26
  46.4 2.0 copy-start
  54.6 0.7 copy-start.4
  54.6 242.9 %reduce-scatter.2.cloned.1.call-start = ((), (), s32[]{:S(2)}) async-start(), calls=%async_computation.1 | async-start | bytes 1179648 | tf_op jit(solution)/shard_map/reduce_scatter | solution.py:41
  253.7 2.0 copy-start.5
Sparse Core Ops, SparseCore 0:
  54.7 198.9 all-reduce.2
  265.5 31.8 reduce-scatter.1
